TPU v7x, 512 devices: a whole 4x4x16 slice. The times are simulated.
512 devices in a mesh: seq: 64 (over y, z), fsdp: 8 (over x, core).
Axes of the slice: x: 4, y: 4, z: 16, core: 2. Of those that a mesh axis runs over, the one named last changes fastest.
Arguments:
- probe_tensor: bfloat16 [8192, 8, 2048], P('seq', 'fsdp'), may hold values from -10 to 10
- matcher_tensor: bfloat16 [8192, 8, 2048], P('seq', 'fsdp'), may hold values from -10 to 10
- payload_tensor: bfloat16 [8192, 8, 2048], P('seq', 'fsdp'), may hold values from -6 to 6
- adjoint_attended: bfloat16 [8192, 8, 2048], P('seq', 'fsdp'), may hold values from -6 to 6
- logit_scale: float32 [16], replicated, may hold values from 0.5 to 2
- anchor_tiles: int32 [16, 2], replicated, may hold values from 0 to 127, as said below
- sampled_tiles: int32 [16, 128, 3], replicated, may hold values from 0 to 127, as said below
Outputs:
- query_gradients: bfloat16 [8192, 8, 2048], P('seq', 'fsdp')
- grad_key: bfloat16 [8192, 8, 2048], P('seq', 'fsdp')
- grad_value: bfloat16 [8192, 8, 2048], P('seq', 'fsdp')
- adjoint_scales: float32 [16], replicated
Inputs may be any that keep to these rules, and one draw needn't show every extreme that they name: `anchor_tiles`: each head lists 2 different blocks. `sampled_tiles`: each row lists 3 different blocks, none within one block of the row's own block and none among the head's global blocks.
All inputs are finite; a program needn't handle non-finite values.
Results may differ from a plain program's by a relative error of at most 0.0083.
Values may be sent and summed in bfloat16 or wider, within the bound.
No kernel may reach another device: no remote copies, remote signals or barrier semaphores. Data moves between devices by JAX's collectives and lax.ppermute only.
A program may use at most 64 MiB of HBM per device.

v0:
```python
import math
import jax
import jax.numpy as jnp
from jax import lax
from jax.sharding import PartitionSpec as P

TILE_SPAN = 64
masked_minimum = -1e30


def group_of():
    for size in (8, 4, 2):
        return size
    return 1


def block_lists(anchor_tiles, sampled_tiles, nblocks):
    channel_roster = anchor_tiles.shape[0]
    block_ids = jnp.arange(nblocks, dtype=jnp.int32)
    offsets = jnp.array([-1, 0, 1], dtype=jnp.int32)
    window = jnp.broadcast_to(
        (block_ids[:, None] + offsets[None, :])[None], (channel_roster, nblocks, 3)
    )
    window_ok = (window >= 0) & (window < nblocks)
    glob_slots = jnp.broadcast_to(
        anchor_tiles[:, None, :], (channel_roster, nblocks, anchor_tiles.shape[1])
    )
    glob_ok = jnp.abs(glob_slots - block_ids[None, :, None]) > 1
    rand_ok = jnp.ones(sampled_tiles.shape, dtype=bool)
    position_pointer = jnp.concatenate([window, glob_slots, sampled_tiles], axis=2)
    position_pointer = jnp.clip(position_pointer, 0, nblocks - 1)
    position_usable = jnp.concatenate([window_ok, glob_ok, rand_ok], axis=2)
    return (position_pointer, position_usable)


def share_units(device_portion, tok_local, seq_parts, copies, tile_index, tile_span):
    piece = tok_local // copies
    per_piece = piece // tile_index
    units = jnp.arange(seq_parts * per_piece, dtype=jnp.int32)
    position = (
        units // per_piece * tok_local + device_portion * piece + units % per_piece * tile_index
    )
    return position // tile_span


def attend_sample(
    probe_vector,
    matcher_tiles,
    payload_tiles,
    adjoint_signal,
    channel_scale,
    position_pointer,
    position_usable,
    tile_index,
    tile_span,
):
    q_len, channel_width = probe_vector.shape
    k_len = matcher_tiles.shape[0]
    q_units = q_len // tile_index
    k_blocks = k_len // tile_span
    group_size = group_of()
    group_count = q_units // group_size
    reciprocal_sqrt_width = 1.0 / math.sqrt(channel_width)
    key_blocks = matcher_tiles.reshape(k_blocks, tile_span, channel_width)
    value_blocks = payload_tiles.reshape(k_blocks, tile_span, channel_width)
    q_groups = probe_vector.reshape(group_count, group_size, tile_index, channel_width)
    g_groups = adjoint_signal.reshape(group_count, group_size, tile_index, channel_width)
    i_groups = position_pointer.reshape(group_count, group_size, -1)
    v_groups = position_usable.reshape(group_count, group_size, -1)

    def step(carried, inputs):
        key_acc, value_acc, temp_acc = carried
        q_blk, g_blk, idx_blk, ok_blk = inputs
        k_sel = key_blocks[idx_blk]
        v_sel = value_blocks[idx_blk]
        logit_matrix = (
            jnp.einsum("gbd,gsjd->gbsj", q_blk, k_sel, preferred_element_type=jnp.float32)
            * reciprocal_sqrt_width
        )
        position_filter = ok_blk[:, None, :, None]
        rescaled_logits = jnp.where(position_filter, channel_scale * logit_matrix, masked_minimum)
        row_max = jnp.max(rescaled_logits, axis=(2, 3), keepdims=True)
        expo_terms = jnp.where(position_filter, jnp.exp(rescaled_logits - row_max), 0.0)
        row_total = jnp.sum(expo_terms, axis=(2, 3), keepdims=True)
        attn_prob = expo_terms / row_total
        prob_low = attn_prob.astype(jnp.bfloat16)
        d_prob = jnp.einsum("gbd,gsjd->gbsj", g_blk, v_sel, preferred_element_type=jnp.float32)
        row_delta = jnp.sum(attn_prob * d_prob, axis=(2, 3), keepdims=True)
        adjoint_weights = attn_prob * (d_prob - row_delta)
        temp_acc = temp_acc + jnp.sum(adjoint_weights * logit_matrix)
        adjoint_logits = (adjoint_weights * (channel_scale * reciprocal_sqrt_width)).astype(
            jnp.bfloat16
        )
        adjoint_probe = jnp.einsum(
            "gbsj,gsjd->gbd", adjoint_logits, k_sel, preferred_element_type=jnp.float32
        )
        d_keys = jnp.einsum(
            "gbsj,gbd->gsjd", adjoint_logits, q_blk, preferred_element_type=jnp.float32
        )
        d_values = jnp.einsum("gbsj,gbd->gsjd", prob_low, g_blk, preferred_element_type=jnp.float32)
        key_acc = key_acc.at[idx_blk].add(d_keys)
        value_acc = value_acc.at[idx_blk].add(d_values)
        return ((key_acc, value_acc, temp_acc), adjoint_probe.astype(jnp.bfloat16))

    start = (
        jnp.zeros((k_blocks, tile_span, channel_width), jnp.float32),
        jnp.zeros((k_blocks, tile_span, channel_width), jnp.float32),
        jnp.zeros((), jnp.float32),
    )
    (key_acc, value_acc, temp_acc), adjoint_probe = lax.scan(
        step, start, (q_groups, g_groups, i_groups, v_groups)
    )
    return (
        adjoint_probe.reshape(q_len, channel_width),
        key_acc.reshape(k_len, channel_width).astype(jnp.bfloat16),
        value_acc.reshape(k_len, channel_width).astype(jnp.bfloat16),
        temp_acc,
    )


def on_device(
    probe_tensor,
    matcher_tensor,
    payload_tensor,
    adjoint_attended,
    logit_scale,
    anchor_tiles,
    sampled_tiles,
):
    tok_local, seq_count, width = probe_tensor.shape
    channel_roster = logit_scale.shape[0]
    channel_width = width // channel_roster
    seq_parts = lax.axis_size("seq")
    item_total = seq_count * channel_roster
    copies = max(1, seq_parts // item_total)
    per_device = max(1, item_total // seq_parts)
    piece = tok_local // copies
    tile_index = min(TILE_SPAN, piece)

    def to_samples(array):
        return jnp.repeat(array.reshape(tok_local, item_total, channel_width), copies, axis=1)

    def to_shares(array):
        split = array.reshape(copies, piece, item_total, channel_width).transpose(1, 2, 0, 3)
        return split.reshape(piece, item_total * copies, channel_width)

    query_send = to_shares(probe_tensor)
    grad_send = to_shares(adjoint_attended)
    query_item = lax.all_to_all(query_send, "seq", split_axis=1, concat_axis=0, tiled=True)
    key_item = lax.all_to_all(
        to_samples(matcher_tensor), "seq", split_axis=1, concat_axis=0, tiled=True
    )
    value_item = lax.all_to_all(
        to_samples(payload_tensor), "seq", split_axis=1, concat_axis=0, tiled=True
    )
    grad_item = lax.all_to_all(grad_send, "seq", split_axis=1, concat_axis=0, tiled=True)
    length = key_item.shape[0]
    nblocks = length // TILE_SPAN
    my_index = lax.axis_index("seq")
    replica = my_index % copies
    position_pointer, position_usable = block_lists(anchor_tiles, sampled_tiles, nblocks)
    first_item = my_index // copies * per_device
    channel_finder = (first_item + jnp.arange(per_device, dtype=jnp.int32)) % channel_roster
    channel_subset = channel_finder[:, None] == jnp.arange(channel_roster, dtype=jnp.int32)[None, :]
    sample_scales = jnp.sum(jnp.where(channel_subset, logit_scale[None, :], 0.0), axis=1)
    item_index = jnp.sum(
        jnp.where(channel_subset[:, :, None, None], position_pointer[None], 0), axis=1
    )
    item_valid = jnp.any(channel_subset[:, :, None, None] & position_usable[None], axis=1)
    tiles_per_device = share_units(replica, tok_local, seq_parts, copies, tile_index, TILE_SPAN)
    item_index = jnp.take(item_index, tiles_per_device, axis=1)
    item_valid = jnp.take(item_valid, tiles_per_device, axis=1)

    def sample_mapped(sample_operands):
        (
            probe_vector,
            matcher_tiles,
            payload_tiles,
            adjoint_signal,
            channel_scale,
            sample_indices,
            sample_valid_mask,
        ) = sample_operands
        return attend_sample(
            probe_vector,
            matcher_tiles,
            payload_tiles,
            adjoint_signal,
            channel_scale,
            sample_indices,
            sample_valid_mask,
            tile_index,
            TILE_SPAN,
        )

    adjoint_probe, adjoint_matcher, adjoint_payload, adjoint_scale = lax.map(
        sample_mapped,
        (
            jnp.moveaxis(query_item, 1, 0),
            jnp.moveaxis(key_item, 1, 0),
            jnp.moveaxis(value_item, 1, 0),
            jnp.moveaxis(grad_item, 1, 0),
            sample_scales,
            item_index,
            item_valid,
        ),
    )
    scale_pieces = jnp.sum(jnp.where(channel_subset, adjoint_scale[:, None], 0.0), axis=0)
    adjoint_scales = lax.psum(scale_pieces, ("seq", "fsdp"))
    query_grad = jnp.moveaxis(adjoint_probe, 0, 1)
    key_send = jnp.moveaxis(adjoint_matcher, 0, 1)
    value_send = jnp.moveaxis(adjoint_payload, 0, 1)
    back_query = lax.all_to_all(query_grad, "seq", split_axis=0, concat_axis=1, tiled=True)
    returned_key = lax.all_to_all(key_send, "seq", split_axis=0, concat_axis=1, tiled=True)
    returned_value = lax.all_to_all(value_send, "seq", split_axis=0, concat_axis=1, tiled=True)

    def combine_portions(received):
        summed = jnp.sum(
            received.astype(jnp.float32).reshape(tok_local, item_total, copies, channel_width),
            axis=2,
        )
        return summed.astype(jnp.bfloat16).reshape(tok_local, seq_count, width)

    query_gradients = (
        back_query.reshape(piece, item_total, copies, channel_width)
        .transpose(2, 0, 1, 3)
        .reshape(tok_local, seq_count, width)
    )
    return (
        query_gradients,
        combine_portions(returned_key),
        combine_portions(returned_value),
        adjoint_scales,
    )


def solution(mesh):
    placed = (
        P("seq", "fsdp", None),
        P("seq", "fsdp", None),
        P("seq", "fsdp", None),
        P("seq", "fsdp", None),
        P(),
        P(),
        P(),
    )
    return jax.shard_map(
        on_device,
        mesh=mesh,
        in_specs=placed,
        out_specs=(P("seq", "fsdp", None), P("seq", "fsdp", None), P("seq", "fsdp", None), P()),
        check_vma=False,
    )
```

profile of v0, /device:TPU:1, one launch (start us, length us, event | category | flops | bytes accessed | tf_op | source)
XLA Modules:
  0.0 966.9 jit_solution(14185936706878660316)
XLA Ops:
  2.8 19.5 %all-to-all-start = ((bf16[32,64,128]{2,0,1:T(8,128)(2,1)}), bf16[32,64,128]{2,0,1:T(8,128)(2,1)}, u32[]{:S(2)}, u32[]{:S(2)}) async-start(bf16[32,64,128]{2,0,1:T(8,128)(2,1)} %bitcast.24), calls=%async_computation | async-start | bytes 1048576 | tf_op jit(solution)/shard_map/all_to_all | solution.py:149
  23.5 28.3 %all-to-all-done = bf16[32,64,128]{2,0,1:T(8,128)(2,1)} async-done(((bf16[32,64,128]{2,0,1:T(8,128)(2,1)}), bf16[32,64,128]{2,0,1:T(8,128)(2,1)}, u32[]{:S(2)}, u32[]{:S(2)}) %all-to-all-start) | async-done | bytes 524320 | tf_op jit(solution)/shard_map/all_to_all | solution.py:149
  51.7 8.8 all-to-all-start.2
  60.8 29.1 %all-to-all-done.2 = bf16[32,64,128]{2,0,1:T(8,128)(2,1)} async-done(((bf16[32,64,128]{2,0,1:T(8,128)(2,1)}), bf16[32,64,128]{2,0,1:T(8,128)(2,1)}, u32[]{:S(2)}, u32[]{:S(2)}) %all-to-all-start.2) | async-done | bytes 524320 | tf_op jit(solution)/shard_map/all_to_all | solution.py:156
  91.7 8.9 all-to-all-start.1
  100.9 91.5 %all-to-all-done.1 = bf16[128,64,128]{2,0,1:T(8,128)(2,1)} async-done(((bf16[128,64,128]{2,0,1:T(8,128)(2,1)}), bf16[128,64,128]{2,0,1:T(8,128)(2,1)}, u32[]{:S(2)}, u32[]{:S(2)}) %all-to-all-start.1) | async-done | bytes 2097184 | tf_op jit(solution)/shard_map/all_to_all | solution.py:150
  194.2 14.3 %all-to-all-start.3 = ((bf16[128,64,128]{2,0,1:T(8,128)(2,1)}), bf16[128,64,128]{2,0,1:T(8,128)(2,1)}, u32[]{:S(2)}, u32[]{:S(2)}) async-start(bf16[128,64,128]{2,0,1:T(8,128)(2,1)} %bitcast.37), calls=%async_computation.3 | async-start | bytes 4194304 | tf_op jit(solution)/shard_map/all_to_all | solution.py:153
  212.1 91.3 %all-to-all-done.3 = bf16[128,64,128]{2,0,1:T(8,128)(2,1)} async-done(((bf16[128,64,128]{2,0,1:T(8,128)(2,1)}), bf16[128,64,128]{2,0,1:T(8,128)(2,1)}, u32[]{:S(2)}, u32[]{:S(2)}) %all-to-all-start.3) | async-done | bytes 2097184 | tf_op jit(solution)/shard_map/all_to_all | solution.py:153
  308.3 305.0 %while.32 = (s32[]{:T(128)}, f32[128,64,128]{2,1,0:T(8,128)}, f32[128,64,128]{2,1,0:T(8,128)}, f32[]{:T(128)}, bf16[8,8,32,128]{3,2,1,0:T(8,128)(2,1)}, /*index=...) while((s32[]{:T(128)}, f32[128,64,128]{2,1,0:T(8,128)}, ...), condition=%wide.region_10.11_spmd, body=%wide.region_3.10_spmd.sunk | while | flops 173179328 | bytes 30234488 | solution.py:110
  316.5 10.3 %scatter_fusion.1 = f32[128,64,128]{2,1,0:T(8,128)} fusion(f32[128,64,128]{2,1,0:T(8,128)} %get-tuple-element.349, s32[64]{0:T(128)S(1)} %reshape.476, f32[64,64,128]{2,1,0:T(8,128)} %bitcast.170), kind=kCustom, calls=%fused_computation.5.clone.1 | custom fusion | flops 524288 | bytes 6291712 | tf_op jit(solution)/shard_map/while/body/eval_jaxpr/while/body/eval_jaxpr/scatter-add | solution.py:102
  334.8 9.1 scatter_fusion
  354.6 10.3 %scatter_fusion.1 = f32[128,64,128]{2,1,0:T(8,128)} fusion(f32[128,64,128]{2,1,0:T(8,128)} %get-tuple-element.349, s32[64]{0:T(128)S(1)} %reshape.476, f32[64,64,128]{2,1,0:T(8,128)} %bitcast.170), kind=kCustom, calls=%fused_computation.5.clone.1 | custom fusion | flops 524288 | bytes 6291712 | tf_op jit(solution)/shard_map/while/body/eval_jaxpr/while/body/eval_jaxpr/scatter-add | solution.py:102
  372.9 9.0 scatter_fusion
  392.7 10.4 %scatter_fusion.1 = f32[128,64,128]{2,1,0:T(8,128)} fusion(f32[128,64,128]{2,1,0:T(8,128)} %get-tuple-element.349, s32[64]{0:T(128)S(1)} %reshape.476, f32[64,64,128]{2,1,0:T(8,128)} %bitcast.170), kind=kCustom, calls=%fused_computation.5.clone.1 | custom fusion | flops 524288 | bytes 6291712 | tf_op jit(solution)/shard_map/while/body/eval_jaxpr/while/body/eval_jaxpr/scatter-add | solution.py:102
  411.1 9.0 scatter_fusion
  430.9 10.4 %scatter_fusion.1 = f32[128,64,128]{2,1,0:T(8,128)} fusion(f32[128,64,128]{2,1,0:T(8,128)} %get-tuple-element.349, s32[64]{0:T(128)S(1)} %reshape.476, f32[64,64,128]{2,1,0:T(8,128)} %bitcast.170), kind=kCustom, calls=%fused_computation.5.clone.1 | custom fusion | flops 524288 | bytes 6291712 | tf_op jit(solution)/shard_map/while/body/eval_jaxpr/while/body/eval_jaxpr/scatter-add | solution.py:102
  449.2 9.1 scatter_fusion
  469.0 10.3 %scatter_fusion.1 = f32[128,64,128]{2,1,0:T(8,128)} fusion(f32[128,64,128]{2,1,0:T(8,128)} %get-tuple-element.349, s32[64]{0:T(128)S(1)} %reshape.476, f32[64,64,128]{2,1,0:T(8,128)} %bitcast.170), kind=kCustom, calls=%fused_computation.5.clone.1 | custom fusion | flops 524288 | bytes 6291712 | tf_op jit(solution)/shard_map/while/body/eval_jaxpr/while/body/eval_jaxpr/scatter-add | solution.py:102
  487.3 9.0 scatter_fusion
  507.1 10.4 %scatter_fusion.1 = f32[128,64,128]{2,1,0:T(8,128)} fusion(f32[128,64,128]{2,1,0:T(8,128)} %get-tuple-element.349, s32[64]{0:T(128)S(1)} %reshape.476, f32[64,64,128]{2,1,0:T(8,128)} %bitcast.170), kind=kCustom, calls=%fused_computation.5.clone.1 | custom fusion | flops 524288 | bytes 6291712 | tf_op jit(solution)/shard_map/while/body/eval_jaxpr/while/body/eval_jaxpr/scatter-add | solution.py:102
  525.5 9.0 scatter_fusion
  545.3 10.4 %scatter_fusion.1 = f32[128,64,128]{2,1,0:T(8,128)} fusion(f32[128,64,128]{2,1,0:T(8,128)} %get-tuple-element.349, s32[64]{0:T(128)S(1)} %reshape.476, f32[64,64,128]{2,1,0:T(8,128)} %bitcast.170), kind=kCustom, calls=%fused_computation.5.clone.1 | custom fusion | flops 524288 | bytes 6291712 | tf_op jit(solution)/shard_map/while/body/eval_jaxpr/while/body/eval_jaxpr/scatter-add | solution.py:102
  563.6 9.1 scatter_fusion
  583.4 10.4 %scatter_fusion.1 = f32[128,64,128]{2,1,0:T(8,128)} fusion(f32[128,64,128]{2,1,0:T(8,128)} %get-tuple-element.349, s32[64]{0:T(128)S(1)} %reshape.476, f32[64,64,128]{2,1,0:T(8,128)} %bitcast.170), kind=kCustom, calls=%fused_computation.5.clone.1 | custom fusion | flops 524288 | bytes 6291712 | tf_op jit(solution)/shard_map/while/body/eval_jaxpr/while/body/eval_jaxpr/scatter-add | solution.py:102
  601.7 9.0 scatter_fusion
  616.9 10.2 %all-to-all-start.4 = ((bf16[64,2,2048]{2,1,0:T(2,128)(2,1)}), bf16[64,2,2048]{2,1,0:T(2,128)(2,1)S(1)}, u32[]{:S(2)}, u32[]{:S(2)}) async-start(bf16[64,2,2048]{2,1,0:T(2,128)(2,1)} %reshape.453), calls=%async_computation.4 | async-start | bytes 1048576 | tf_op jit(solution)/shard_map/all_to_all | solution.py:213
  636.7 20.0 %all-to-all-done.4 = bf16[64,2,2048]{2,1,0:T(2,128)(2,1)S(1)} async-done(((bf16[64,2,2048]{2,1,0:T(2,128)(2,1)}), bf16[64,2,2048]{2,1,0:T(2,128)(2,1)S(1)}, u32[]{:S(2)}, u32[]{:S(2)}) %all-to-all-start.4) | async-done | bytes 524320 | tf_op jit(solution)/shard_map/all_to_all | solution.py:213
  657.4 8.8 all-to-all-start.5
  678.7 78.7 %all-to-all-done.5 = bf16[64,2,8192]{2,1,0:T(2,128)(2,1)S(1)} async-done(((bf16[64,2,8192]{2,1,0:T(2,128)(2,1)}), bf16[64,2,8192]{2,1,0:T(2,128)(2,1)S(1)}, u32[]{:S(2)}, u32[]{:S(2)}) %all-to-all-start.5) | async-done | bytes 2097184 | tf_op jit(solution)/shard_map/all_to_all | solution.py:214
  757.4 14.3 %all-to-all-start.6 = ((bf16[64,2,8192]{2,1,0:T(2,128)(2,1)}), bf16[64,2,8192]{2,1,0:T(2,128)(2,1)}, u32[]{:S(2)}, u32[]{:S(2)}) async-start(bf16[64,2,8192]{2,1,0:T(2,128)(2,1)} %reshape.457), calls=%async_computation.6 | async-start | bytes 4194304 | tf_op jit(solution)/shard_map/all_to_all | solution.py:215
  771.7 164.4 %psum.7 = f32[16]{0:T(128)} all-reduce(f32[16]{0:T(128)S(1)} %broadcast_select_fusion), channel_id=1, replica_groups=mesh['seq'=64,'fsdp'=8] {'seq','fsdp'}, use_global_device_ids=true, to_apply=%region_13.14 | all-reduce | flops 16 | bytes 128 | tf_op jit(solution)/shard_map/psum | solution.py:209
  952.2 10.4 %reshape.458 = bf16[8192,1,128]{2,1,0:T(2,128)(2,1)} reshape(bf16[64,2,8192]{2,1,0:T(2,128)(2,1)} %all-to-all-done.6) | data formatting | bytes 4194304
  (196 shorter events, 206.1 us)
Async XLA Ops:
  0.6 21.7 %copy-start.2 = (bf16[128,1,2048]{2,0,1:T(8,128)(2,1)S(1)}, bf16[128,1,2048]{2,0,1:T(8,128)(2,1)}, u32[]{:S(2)}) copy-start(bf16[128,1,2048]{2,0,1:T(8,128)(2,1)} %param.13) | copy-start | bytes 1572868
  2.8 48.9 %all-to-all-start = ((bf16[32,64,128]{2,0,1:T(8,128)(2,1)}), bf16[32,64,128]{2,0,1:T(8,128)(2,1)}, u32[]{:S(2)}, u32[]{:S(2)}) async-start(bf16[32,64,128]{2,0,1:T(8,128)(2,1)} %bitcast.24), calls=%async_computation | async-start | bytes 1048576 | tf_op jit(solution)/shard_map/all_to_all | solution.py:149
  22.4 38.2 %copy-start.3 = (bf16[128,1,2048]{2,0,1:T(8,128)(2,1)S(1)}, bf16[128,1,2048]{2,0,1:T(8,128)(2,1)}, u32[]{:S(2)}) copy-start(bf16[128,1,2048]{2,0,1:T(8,128)(2,1)} %param.11) | copy-start | bytes 1572868
  51.7 38.1 %all-to-all-start.2 = ((bf16[32,64,128]{2,0,1:T(8,128)(2,1)}), bf16[32,64,128]{2,0,1:T(8,128)(2,1)}, u32[]{:S(2)}, u32[]{:S(2)}) async-start(bf16[32,64,128]{2,0,1:T(8,128)(2,1)} %bitcast.33), calls=%async_computation.2 | async-start | bytes 1048576 | tf_op jit(solution)/shard_map/all_to_all | solution.py:156
  91.7 8.9 copy-start.4
  91.7 100.6 %all-to-all-start.1 = ((bf16[128,64,128]{2,0,1:T(8,128)(2,1)}), bf16[128,64,128]{2,0,1:T(8,128)(2,1)}, u32[]{:S(2)}, u32[]{:S(2)}) async-start(bf16[128,64,128]{2,0,1:T(8,128)(2,1)} %bitcast.28), calls=%async_computation.1 | async-start | bytes 4194304 | tf_op jit(solution)/shard_map/all_to_all | solution.py:150
  194.2 14.4 %copy-start.7 = (s32[3]{0:T(128)S(1)}, s32[3]{0:T(128)}, u32[]{:S(2)}) copy-start(s32[3]{0:T(128)} %constant.217.clone) | copy-start | bytes 40
  194.2 14.5 %copy-start.6 = (s32[16,2]{0,1:T(2,128)S(1)}, s32[16,2]{0,1:T(2,128)}, u32[]{:S(2)}) copy-start(s32[16,2]{0,1:T(2,128)} %param.15) | copy-start | bytes 388
  194.2 14.6 %copy-start.5 = (s32[16,128,3]{1,0,2:T(8,128)S(1)}, s32[16,128,3]{1,0,2:T(8,128)}, u32[]{:S(2)}) copy-start(s32[16,128,3]{1,0,2:T(8,128)} %param.16) | copy-start | bytes 73732
  194.2 16.5 %copy-start.8 = (f32[16]{0:T(128)S(1)}, f32[16]{0:T(128)}, u32[]{:S(2)}) copy-start(f32[16]{0:T(128)} %param.14) | copy-start | bytes 196
  194.2 109.2 %all-to-all-start.3 = ((bf16[128,64,128]{2,0,1:T(8,128)(2,1)}), bf16[128,64,128]{2,0,1:T(8,128)(2,1)}, u32[]{:S(2)}, u32[]{:S(2)}) async-start(bf16[128,64,128]{2,0,1:T(8,128)(2,1)} %bitcast.37), calls=%async_computation.3 | async-start | bytes 4194304 | tf_op jit(solution)/shard_map/all_to_all | solution.py:153
  332.6 0.8 copy-start
  370.8 0.8 copy-start
  408.9 0.8 copy-start
  447.0 0.8 copy-start
  485.2 0.8 copy-start
  523.3 0.8 copy-start
  561.4 0.8 copy-start
  599.6 0.8 copy-start
  616.9 39.7 %all-to-all-start.4 = ((bf16[64,2,2048]{2,1,0:T(2,128)(2,1)}), bf16[64,2,2048]{2,1,0:T(2,128)(2,1)S(1)}, u32[]{:S(2)}, u32[]{:S(2)}) async-start(bf16[64,2,2048]{2,1,0:T(2,128)(2,1)} %reshape.453), calls=%async_computation.4 | async-start | bytes 1048576 | tf_op jit(solution)/shard_map/all_to_all | solution.py:213
  656.6 0.8 copy-start.1
  657.4 100.0 %all-to-all-start.5 = ((bf16[64,2,8192]{2,1,0:T(2,128)(2,1)}), bf16[64,2,8192]{2,1,0:T(2,128)(2,1)S(1)}, u32[]{:S(2)}, u32[]{:S(2)}) async-start(bf16[64,2,8192]{2,1,0:T(2,128)(2,1)} %reshape.455), calls=%async_computation.5 | async-start | bytes 4194304 | tf_op jit(solution)/shard_map/all_to_all | solution.py:214
  757.4 194.8 %all-to-all-start.6 = ((bf16[64,2,8192]{2,1,0:T(2,128)(2,1)}), bf16[64,2,8192]{2,1,0:T(2,128)(2,1)}, u32[]{:S(2)}, u32[]{:S(2)}) async-start(bf16[64,2,8192]{2,1,0:T(2,128)(2,1)} %reshape.457), calls=%async_computation.6 | async-start | bytes 4194304 | tf_op jit(solution)/shard_map/all_to_all | solution.py:215
where the time goes:
time: 975 us; the launch traced here: 967 us
  waiting for transfers between devices  339 us (35%)
  other arithmetic  189 us (19%)
  blocking collectives  164 us (17%)
  local copies, waits for them, and re-layouts  98.4 us (10%)
  starting transfers between devices  84.8 us (9%)
  matrix products  84.5 us (9%)
    psum x1, blocking collectives, on_device(): adjoint_scales = lax.psum(scale_pieces, ('seq', 'fsdp'))  164 us
    all_to_all x1, waiting for transfers between devices, on_device(): lax.all_to_all(to_samples(matcher_tensor), 'seq', split_axis=1, concat_ax...  91.5 us
    all_to_all x1, waiting for transfers between devices, on_device(): lax.all_to_all(to_samples(payload_tensor), 'seq', split_axis=1, concat_ax...  91.3 us
    scatter-add x8, other arithmetic, step(): value_acc = value_acc.at[idx_blk].add(d_values)  82.8 us
    all_to_all x1, waiting for transfers between devices, on_device(): lax.all_to_all(key_send, 'seq', split_axis=0, concat_axis=1, tiled=True)  78.7 us
    scatter-add x8, other arithmetic, step(): key_acc = key_acc.at[idx_blk].add(d_keys)  72.5 us
    unnamed x31, local copies, waits for them, and re-layouts  39 us
    all_to_all x1, waiting for transfers between devices, on_device(): lax.all_to_all(grad_send, 'seq', split_axis=1, concat_axis=0, tiled=True)  29.1 us
  transfers between devices with their start and end apart: 7, of which 6 were waited for; matrix products, arithmetic and copies ran while one was open for 4% of the time, Pallas kernels for 0%

commit v1 on v0

--- a/solution.py
+++ b/solution.py
@@ -206,7 +206,8 @@
         ),
     )
     scale_pieces = jnp.sum(jnp.where(channel_subset, adjoint_scale[:, None], 0.0), axis=0)
-    adjoint_scales = lax.psum(scale_pieces, ("seq", "fsdp"))
+    half = lax.psum(scale_pieces, "seq")
+    adjoint_scales = lax.psum(half, "fsdp")
     query_grad = jnp.moveaxis(adjoint_probe, 0, 1)
     key_send = jnp.moveaxis(adjoint_matcher, 0, 1)
     value_send = jnp.moveaxis(adjoint_payload, 0, 1)

time: 975 us -> 1050 us (1.077)
  blocking collectives: 164 us -> 238 us
    psum x1 -> x2, blocking collectives: 164 us -> 238 us  [the longest x1 197 us: on_device(): half = lax.psum(scale_pieces, 'seq')]
where the time goes in v1:
time: 1050 us; the launch traced here: 1040 us
  waiting for transfers between devices  339 us (32%)
  blocking collectives  238 us (23%)
  other arithmetic  189 us (18%)
  local copies, waits for them, and re-layouts  98.4 us (9%)
  starting transfers between devices  84.8 us (8%)
  matrix products  84.5 us (8%)
    psum x1, blocking collectives, on_device(): half = lax.psum(scale_pieces, 'seq')  197 us
    all_to_all x1, waiting for transfers between devices, on_device(): lax.all_to_all(to_samples(matcher_tensor), 'seq', split_axis=1, concat_ax...  91.5 us
    all_to_all x1, waiting for transfers between devices, on_device(): lax.all_to_all(to_samples(payload_tensor), 'seq', split_axis=1, concat_ax...  91.3 us
    scatter-add x8, other arithmetic, step(): value_acc = value_acc.at[idx_blk].add(d_values)  82.8 us
    all_to_all x1, waiting for transfers between devices, on_device(): lax.all_to_all(key_send, 'seq', split_axis=0, concat_axis=1, tiled=True)  78.7 us
    scatter-add x8, other arithmetic, step(): key_acc = key_acc.at[idx_blk].add(d_keys)  72.5 us
    psum x1, blocking collectives, on_device(): adjoint_scales = lax.psum(half, 'fsdp')  40.7 us
    unnamed x31, local copies, waits for them, and re-layouts  39 us
  transfers between devices with their start and end apart: 7, of which 6 were waited for; matrix products, arithmetic and copies ran while one was open for 4% of the time, Pallas kernels for 0%

profile of v1, /device:TPU:1, one launch (start us, length us, event | category | flops | bytes accessed | tf_op | source)
XLA Modules:
  0.0 1040.2 jit_solution(6756276460864452721)
XLA Ops:
  2.8 19.5 %all-to-all-start = ((bf16[32,64,128]{2,0,1:T(8,128)(2,1)}), bf16[32,64,128]{2,0,1:T(8,128)(2,1)}, u32[]{:S(2)}, u32[]{:S(2)}) async-start(bf16[32,64,128]{2,0,1:T(8,128)(2,1)} %bitcast.24), calls=%async_computation | async-start | bytes 1048576 | tf_op jit(solution)/shard_map/all_to_all | solution.py:149
  23.5 28.3 %all-to-all-done = bf16[32,64,128]{2,0,1:T(8,128)(2,1)} async-done(((bf16[32,64,128]{2,0,1:T(8,128)(2,1)}), bf16[32,64,128]{2,0,1:T(8,128)(2,1)}, u32[]{:S(2)}, u32[]{:S(2)}) %all-to-all-start) | async-done | bytes 524320 | tf_op jit(solution)/shard_map/all_to_all | solution.py:149
  51.7 8.8 all-to-all-start.2
  60.8 29.1 %all-to-all-done.2 = bf16[32,64,128]{2,0,1:T(8,128)(2,1)} async-done(((bf16[32,64,128]{2,0,1:T(8,128)(2,1)}), bf16[32,64,128]{2,0,1:T(8,128)(2,1)}, u32[]{:S(2)}, u32[]{:S(2)}) %all-to-all-start.2) | async-done | bytes 524320 | tf_op jit(solution)/shard_map/all_to_all | solution.py:156
  91.7 8.9 all-to-all-start.1
  100.9 91.5 %all-to-all-done.1 = bf16[128,64,128]{2,0,1:T(8,128)(2,1)} async-done(((bf16[128,64,128]{2,0,1:T(8,128)(2,1)}), bf16[128,64,128]{2,0,1:T(8,128)(2,1)}, u32[]{:S(2)}, u32[]{:S(2)}) %all-to-all-start.1) | async-done | bytes 2097184 | tf_op jit(solution)/shard_map/all_to_all | solution.py:150
  194.2 14.3 %all-to-all-start.3 = ((bf16[128,64,128]{2,0,1:T(8,128)(2,1)}), bf16[128,64,128]{2,0,1:T(8,128)(2,1)}, u32[]{:S(2)}, u32[]{:S(2)}) async-start(bf16[128,64,128]{2,0,1:T(8,128)(2,1)} %bitcast.37), calls=%async_computation.3 | async-start | bytes 4194304 | tf_op jit(solution)/shard_map/all_to_all | solution.py:153
  212.1 91.3 %all-to-all-done.3 = bf16[128,64,128]{2,0,1:T(8,128)(2,1)} async-done(((bf16[128,64,128]{2,0,1:T(8,128)(2,1)}), bf16[128,64,128]{2,0,1:T(8,128)(2,1)}, u32[]{:S(2)}, u32[]{:S(2)}) %all-to-all-start.3) | async-done | bytes 2097184 | tf_op jit(solution)/shard_map/all_to_all | solution.py:153
  308.3 305.0 %while.32 = (s32[]{:T(128)}, f32[128,64,128]{2,1,0:T(8,128)}, f32[128,64,128]{2,1,0:T(8,128)}, f32[]{:T(128)}, bf16[8,8,32,128]{3,2,1,0:T(8,128)(2,1)}, /*index=...) while((s32[]{:T(128)}, f32[128,64,128]{2,1,0:T(8,128)}, ...), condition=%wide.region_10.11_spmd, body=%wide.region_3.10_spmd.sunk | while | flops 173179328 | bytes 30234488 | solution.py:110
  316.5 10.3 scatter_fusion.1
  334.8 9.1 scatter_fusion
  354.6 10.3 scatter_fusion.1
  372.9 9.0 scatter_fusion
  392.7 10.4 scatter_fusion.1
  411.1 9.0 scatter_fusion
  430.9 10.4 scatter_fusion.1
  449.2 9.1 scatter_fusion
  469.0 10.3 scatter_fusion.1
  487.3 9.0 scatter_fusion
  507.1 10.4 scatter_fusion.1
  525.5 9.0 scatter_fusion
  545.3 10.4 scatter_fusion.1
  563.6 9.1 scatter_fusion
  583.4 10.4 scatter_fusion.1
  601.7 9.0 scatter_fusion
  616.9 10.2 all-to-all-start.4
  636.7 20.0 %all-to-all-done.4 = bf16[64,2,2048]{2,1,0:T(2,128)(2,1)S(1)} async-done(((bf16[64,2,2048]{2,1,0:T(2,128)(2,1)}), bf16[64,2,2048]{2,1,0:T(2,128)(2,1)S(1)}, u32[]{:S(2)}, u32[]{:S(2)}) %all-to-all-start.4) | async-done | bytes 524320 | tf_op jit(solution)/shard_map/all_to_all | solution.py:214
  678.7 78.7 %all-to-all-done.5 = bf16[64,2,8192]{2,1,0:T(2,128)(2,1)S(1)} async-done(((bf16[64,2,8192]{2,1,0:T(2,128)(2,1)}), bf16[64,2,8192]{2,1,0:T(2,128)(2,1)S(1)}, u32[]{:S(2)}, u32[]{:S(2)}) %all-to-all-start.5) | async-done | bytes 2097184 | tf_op jit(solution)/shard_map/all_to_all | solution.py:215
  757.4 14.3 %all-to-all-start.6 = ((bf16[64,2,8192]{2,1,0:T(2,128)(2,1)}), bf16[64,2,8192]{2,1,0:T(2,128)(2,1)}, u32[]{:S(2)}, u32[]{:S(2)}) async-start(bf16[64,2,8192]{2,1,0:T(2,128)(2,1)} %reshape.457), calls=%async_computation.6 | async-start | bytes 4194304 | tf_op jit(solution)/shard_map/all_to_all | solution.py:216
  771.7 197.0 %psum.14 = f32[16]{0:T(128)S(1)} all-reduce(f32[16]{0:T(128)S(1)} %broadcast_select_fusion), channel_id=1, replica_groups=mesh['seq'=64,'fsdp'=8] {'seq'}, use_global_device_ids=true, to_apply=%region_13.14 | all-reduce | flops 16 | bytes 128 | tf_op jit(solution)/shard_map/psum | solution.py:209
  968.7 40.7 %psum.15 = f32[16]{0:T(128)} all-reduce(f32[16]{0:T(128)S(1)} %psum.14), channel_id=1, replica_groups=mesh['seq'=64,'fsdp'=8] {'fsdp'}, use_global_device_ids=true, to_apply=%region_14.15 | all-reduce | flops 16 | bytes 128 | tf_op jit(solution)/shard_map/psum | solution.py:210
  1025.5 10.4 %reshape.458 = bf16[8192,1,128]{2,1,0:T(2,128)(2,1)} reshape(bf16[64,2,8192]{2,1,0:T(2,128)(2,1)} %all-to-all-done.6) | data formatting | bytes 4194304
  (197 shorter events, 214.9 us)
Async XLA Ops:
  0.6 21.7 %copy-start.2 = (bf16[128,1,2048]{2,0,1:T(8,128)(2,1)S(1)}, bf16[128,1,2048]{2,0,1:T(8,128)(2,1)}, u32[]{:S(2)}) copy-start(bf16[128,1,2048]{2,0,1:T(8,128)(2,1)} %param.13) | copy-start | bytes 1572868
  2.8 48.9 %all-to-all-start = ((bf16[32,64,128]{2,0,1:T(8,128)(2,1)}), bf16[32,64,128]{2,0,1:T(8,128)(2,1)}, u32[]{:S(2)}, u32[]{:S(2)}) async-start(bf16[32,64,128]{2,0,1:T(8,128)(2,1)} %bitcast.24), calls=%async_computation | async-start | bytes 1048576 | tf_op jit(solution)/shard_map/all_to_all | solution.py:149
  22.4 38.2 %copy-start.3 = (bf16[128,1,2048]{2,0,1:T(8,128)(2,1)S(1)}, bf16[128,1,2048]{2,0,1:T(8,128)(2,1)}, u32[]{:S(2)}) copy-start(bf16[128,1,2048]{2,0,1:T(8,128)(2,1)} %param.11) | copy-start | bytes 1572868
  51.7 38.1 %all-to-all-start.2 = ((bf16[32,64,128]{2,0,1:T(8,128)(2,1)}), bf16[32,64,128]{2,0,1:T(8,128)(2,1)}, u32[]{:S(2)}, u32[]{:S(2)}) async-start(bf16[32,64,128]{2,0,1:T(8,128)(2,1)} %bitcast.33), calls=%async_computation.2 | async-start | bytes 1048576 | tf_op jit(solution)/shard_map/all_to_all | solution.py:156
  91.7 8.9 copy-start.4
  91.7 100.6 %all-to-all-start.1 = ((bf16[128,64,128]{2,0,1:T(8,128)(2,1)}), bf16[128,64,128]{2,0,1:T(8,128)(2,1)}, u32[]{:S(2)}, u32[]{:S(2)}) async-start(bf16[128,64,128]{2,0,1:T(8,128)(2,1)} %bitcast.28), calls=%async_computation.1 | async-start | bytes 4194304 | tf_op jit(solution)/shard_map/all_to_all | solution.py:150
  194.2 14.4 %copy-start.7 = (s32[3]{0:T(128)S(1)}, s32[3]{0:T(128)}, u32[]{:S(2)}) copy-start(s32[3]{0:T(128)} %constant.217.clone) | copy-start | bytes 40
  194.2 14.5 %copy-start.6 = (s32[16,2]{0,1:T(2,128)S(1)}, s32[16,2]{0,1:T(2,128)}, u32[]{:S(2)}) copy-start(s32[16,2]{0,1:T(2,128)} %param.15) | copy-start | bytes 388
  194.2 14.6 %copy-start.5 = (s32[16,128,3]{1,0,2:T(8,128)S(1)}, s32[16,128,3]{1,0,2:T(8,128)}, u32[]{:S(2)}) copy-start(s32[16,128,3]{1,0,2:T(8,128)} %param.16) | copy-start | bytes 73732
  194.2 16.5 %copy-start.8 = (f32[16]{0:T(128)S(1)}, f32[16]{0:T(128)}, u32[]{:S(2)}) copy-start(f32[16]{0:T(128)} %param.14) | copy-start | bytes 196
  194.2 109.2 %all-to-all-start.3 = ((bf16[128,64,128]{2,0,1:T(8,128)(2,1)}), bf16[128,64,128]{2,0,1:T(8,128)(2,1)}, u32[]{:S(2)}, u32[]{:S(2)}) async-start(bf16[128,64,128]{2,0,1:T(8,128)(2,1)} %bitcast.37), calls=%async_computation.3 | async-start | bytes 4194304 | tf_op jit(solution)/shard_map/all_to_all | solution.py:153
  332.6 0.8 copy-start
  370.8 0.8 copy-start
  408.9 0.8 copy-start
  447.0 0.8 copy-start
  485.2 0.8 copy-start
  523.3 0.8 copy-start
  561.4 0.8 copy-start
  599.6 0.8 copy-start
  616.9 39.7 %all-to-all-start.4 = ((bf16[64,2,2048]{2,1,0:T(2,128)(2,1)}), bf16[64,2,2048]{2,1,0:T(2,128)(2,1)S(1)}, u32[]{:S(2)}, u32[]{:S(2)}) async-start(bf16[64,2,2048]{2,1,0:T(2,128)(2,1)} %reshape.453), calls=%async_computation.4 | async-start | bytes 1048576 | tf_op jit(solution)/shard_map/all_to_all | solution.py:214
  656.6 0.8 copy-start.1
  657.4 100.0 %all-to-all-start.5 = ((bf16[64,2,8192]{2,1,0:T(2,128)(2,1)}), bf16[64,2,8192]{2,1,0:T(2,128)(2,1)S(1)}, u32[]{:S(2)}, u32[]{:S(2)}) async-start(bf16[64,2,8192]{2,1,0:T(2,128)(2,1)} %reshape.455), calls=%async_computation.5 | async-start | bytes 4194304 | tf_op jit(solution)/shard_map/all_to_all | solution.py:215
  757.4 268.1 %all-to-all-start.6 = ((bf16[64,2,8192]{2,1,0:T(2,128)(2,1)}), bf16[64,2,8192]{2,1,0:T(2,128)(2,1)}, u32[]{:S(2)}, u32[]{:S(2)}) async-start(bf16[64,2,8192]{2,1,0:T(2,128)(2,1)} %reshape.457), calls=%async_computation.6 | async-start | bytes 4194304 | tf_op jit(solution)/shard_map/all_to_all | solution.py:216
